TPU v7x, 128 devices: a whole 4x4x4 slice. The times are simulated.
128 devices in a mesh: seq: 32 (over x_hi, z, y), tensor: 2 (over core), dp: 2 (over x_lo).
Axes of the slice: x: 4 (x_hi: 2, x_lo: 2; x = x_hi * 2 + x_lo), y: 4, z: 4, core: 2. Of those that a mesh axis runs over, the one named last changes fastest.
Arguments:
- inputs: bfloat16 [2, 24576, 1536], P('dp', 'seq', 'tensor'), may hold values from -6 to 6
- lengths: int32 [2], P('dp'), may hold values from 6144 to 24576, as said below
- cotangent: bfloat16 [2, 24576, 1536], P('dp', 'seq', 'tensor'), may hold values from -6 to 6
- w_value: bfloat16 [1536, 1536], P(None, 'tensor'), may hold values from -0.15625 to 0.15625
- w_gate: bfloat16 [1536, 1536], P(None, 'tensor'), may hold values from -0.15625 to 0.15625
- kernel: bfloat16 [31, 1536], P(None, 'tensor'), may hold values from -1 to 1
- w_out: bfloat16 [1536, 1536], P('tensor'), may hold values from -0.15625 to 0.15625
Outputs:
- output: bfloat16 [2, 24576, 1536], P('dp', 'seq', 'tensor')
- input_gradient: bfloat16 [2, 24576, 1536], P('dp', 'seq', 'tensor')
- value_grad: float32 [1536, 1536], P(('seq', 'dp'), 'tensor')
- gate_grad: float32 [1536, 1536], P(('seq', 'dp'), 'tensor')
- kernel_grad: float32 [31, 1536], P(None, 'tensor')
- out_grad: float32 [1536, 1536], P('tensor', ('seq', 'dp'))
Inputs may be any that keep to these rules, and one draw needn't show every extreme that they name: `lengths`: in every draw some utterance has all 24576 frames valid.
All inputs are finite; a program needn't handle non-finite values.
Results may differ from a plain program's by a relative error of at most 0.009.
Values may be sent and summed in bfloat16 or wider, within the bound.
A program may use at most 128 MiB of HBM per device.

v0:
```python
import jax
import jax.numpy as jnp
from jax import lax
from jax.sharding import PartitionSpec as P

epsilon = 1e-05


def padded_2(shard, sides, width):
    for axis, dim in sides:
        peers, length = (lax.axis_size(axis), shard.shape[dim])
        up = [(i, (i + 1) % peers) for i in range(peers - 1)]
        down = [(j, i) for i, j in up]
        last = lax.slice_in_dim(shard, length - width, length, axis=dim)
        leading = lax.slice_in_dim(shard, 0, width, axis=dim)
        before = lax.ppermute(last, axis, up)
        after = lax.ppermute(leading, axis, down)
        shard = jnp.concatenate([before, shard, after], axis=dim)
    return shard


def layer_normalizer(values):
    center = values - jnp.mean(values, axis=-1, keepdims=True)
    inverse = lax.rsqrt(jnp.mean(center * center, axis=-1, keepdims=True) + epsilon)
    return (center * inverse, inverse)


def shards(inputs, lengths, cotangent, w_value, w_gate, kernel, w_out):
    frame_total = inputs[0]
    count = frame_total.shape[0]
    channel_total = frame_total.shape[1]
    channel_width = channel_total * lax.axis_size("tensor")
    taps_count = kernel.shape[0]
    half = (taps_count - 1) // 2
    tensor_position = lax.axis_index("tensor")
    first_frame = lax.axis_index("seq") * count
    positions = first_frame + jnp.arange(count, dtype=jnp.int32)
    valid = (positions < lengths[0]).astype(jnp.float32)[:, None]
    taps = kernel.astype(jnp.float32)
    complete_rows = lax.all_gather(frame_total, "tensor", axis=1, tiled=True)
    centered_scaled, inverse_deviation_one = layer_normalizer(complete_rows.astype(jnp.float32))
    normalized_rows = centered_scaled.astype(jnp.bfloat16)
    values = jnp.dot(normalized_rows, w_value, preferred_element_type=jnp.float32)
    gates = jnp.dot(normalized_rows, w_gate, preferred_element_type=jnp.float32)
    sigma = jax.nn.sigmoid(gates)
    hidden = (values * sigma * valid).astype(jnp.bfloat16)
    padded = padded_2(hidden, (("seq", 0),), half).astype(jnp.float32)
    conv = jnp.zeros((count, channel_total), jnp.float32)
    for offset in range(taps_count):
        conv = conv + padded[offset : offset + count] * taps[offset]
    conv_sum, conv_square = lax.psum(
        (jnp.sum(conv, axis=-1), jnp.sum(conv * conv, axis=-1)), "tensor"
    )
    conv_mean = (conv_sum / channel_width)[:, None]
    conv_var = (conv_square / channel_width)[:, None] - conv_mean * conv_mean
    rstd_two = lax.rsqrt(conv_var + epsilon)
    zhat = (conv - conv_mean) * rstd_two
    swish_gate = jax.nn.sigmoid(zhat)
    swished = (zhat * swish_gate).astype(jnp.bfloat16)
    partial_out = jnp.dot(swished, w_out, preferred_element_type=jnp.float32)
    summed = lax.psum_scatter(
        partial_out.astype(jnp.bfloat16), "tensor", scatter_dimension=1, tiled=True
    ).astype(jnp.float32)
    output = (frame_total.astype(jnp.float32) + summed).astype(jnp.bfloat16)
    upstream = cotangent[0]
    upstream_whole = lax.all_gather(upstream, "tensor", axis=1, tiled=True)
    out_term = jnp.dot(swished.T, upstream_whole, preferred_element_type=jnp.float32)
    dswish = jnp.dot(upstream_whole, w_out.T, preferred_element_type=jnp.float32)
    dswish = dswish * (swish_gate + zhat * swish_gate * (1.0 - swish_gate))
    slope_sum, slope_cross = lax.psum(
        (jnp.sum(dswish, axis=-1), jnp.sum(dswish * zhat, axis=-1)), "tensor"
    )
    dconv = rstd_two * (
        dswish
        - (slope_sum / channel_width)[:, None]
        - zhat * (slope_cross / channel_width)[:, None]
    )
    dconv = dconv.astype(jnp.bfloat16)
    slope = dconv.astype(jnp.float32)
    kernel_term = jnp.stack(
        [jnp.sum(padded[offset : offset + count] * slope, axis=0) for offset in range(taps_count)]
    )
    slope_pad = padded_2(dconv, (("seq", 0),), half).astype(jnp.float32)
    dhidden = jnp.zeros((count, channel_total), jnp.float32)
    for offset in range(taps_count):
        dhidden = dhidden + slope_pad[2 * half - offset : 2 * half - offset + count] * taps[offset]
    dhidden = dhidden * valid
    dvalues = (dhidden * sigma).astype(jnp.bfloat16)
    dgates = (dhidden * values * sigma * (1.0 - sigma)).astype(jnp.bfloat16)
    value_term = jnp.dot(normalized_rows.T, dvalues, preferred_element_type=jnp.float32)
    gate_term = jnp.dot(normalized_rows.T, dgates, preferred_element_type=jnp.float32)
    kernel_grad = lax.psum(kernel_term, ("seq", "dp"))
    dnormed_part = jnp.dot(dvalues, w_value.T, preferred_element_type=jnp.float32) + jnp.dot(
        dgates, w_gate.T, preferred_element_type=jnp.float32
    )
    normalized_grad = lax.psum_scatter(
        dnormed_part.astype(jnp.bfloat16), "tensor", scatter_dimension=1, tiled=True
    ).astype(jnp.float32)
    local_centered_scaled = lax.dynamic_slice_in_dim(
        centered_scaled, tensor_position * channel_total, channel_total, 1
    )
    input_total_sum, input_cross_term = lax.psum(
        (
            jnp.sum(normalized_grad, axis=-1),
            jnp.sum(normalized_grad * local_centered_scaled, axis=-1),
        ),
        "tensor",
    )
    input_gradient = upstream.astype(jnp.float32) + inverse_deviation_one * (
        normalized_grad
        - (input_total_sum / channel_width)[:, None]
        - local_centered_scaled * (input_cross_term / channel_width)[:, None]
    )
    input_gradient = input_gradient.astype(jnp.bfloat16)
    value_grad, gate_grad, out_grad = (
        lax.psum_scatter(value_term, ("seq", "dp"), scatter_dimension=0, tiled=True),
        lax.psum_scatter(gate_term, ("seq", "dp"), scatter_dimension=0, tiled=True),
        lax.psum_scatter(out_term, ("seq", "dp"), scatter_dimension=1, tiled=True),
    )
    return (output[None], input_gradient[None], value_grad, gate_grad, kernel_grad, out_grad)


def solution(mesh):
    return jax.shard_map(
        shards,
        mesh=mesh,
        in_specs=(
            P("dp", "seq", "tensor"),
            P("dp"),
            P("dp", "seq", "tensor"),
            P(None, "tensor"),
            P(None, "tensor"),
            P(None, "tensor"),
            P("tensor", None),
        ),
        out_specs=(
            P("dp", "seq", "tensor"),
            P("dp", "seq", "tensor"),
            P(("seq", "dp"), "tensor"),
            P(("seq", "dp"), "tensor"),
            P(None, "tensor"),
            P("tensor", ("seq", "dp")),
        ),
        check_vma=False,
    )
```

profile of v0, /device:TPU:0, one launch (start us, length us, event | category | flops | bytes accessed | tf_op | source)
XLA Modules:
  0.0 1369.6 jit_solution(1484095070607599668)
XLA Ops:
  9.8 16.1 %all-gather.5.cloned.1.call-done = bf16[1,768,1536]{2,1,0:T(8,128)(2,1)} async-done(((bf16[1,768,768]{2,1,0:T(8,128)(2,1)}), bf16[1,768,1536]{2,1,0:T(8,128)(2,1)}) %all-gather.5.cloned.1.call-update) | async-done | bytes 2359312 | tf_op jit(solution)/shard_map/all_gather | solution.py:40
  31.4 3.5 multiply_convert_fusion.3
  34.9 3.5 collective-permute-start
  39.9 4.2 collective-permute-done.1
  44.5 10.7 fusion.94
  57.9 7.0 fusion.93
  67.5 27.0 %fusion.39 = (f32[768]{0:T(1024)}, f32[768]{0:T(1024)}, f32[768]{0:T(1024)}, f32[768]{0:T(1024)}, f32[768]{0:T(1024)}, /*index=5*/f32[768]{0:T(1024)}, f32[768]{...) fusion(f32[798,768]{1,0:T(8,128)} %copy-done.1, ...), kind=kLoop, calls=%fused_computation.77 | loop fusion | flops 25938432 | bytes 48433152 | tf_op jit(solution)/shard_map/reduce_sum | solution.py:81
  95.1 4.0 collective-permute-start.2
  100.4 3.9 convolution_convert_fusion
  106.5 10.9 multiply_convert_fusion
  119.9 3.5 add_convert_fusion
  123.9 15.4 %fusion.38 = (f32[768]{0:T(1024)S(1)}, f32[768]{0:T(1024)S(1)}, f32[768]{0:T(1024)S(1)}, f32[768]{0:T(1024)S(1)}, f32[768]{0:T(1024)S(1)}, /*index=5*/f32[768]{0...) fusion(bf16[768,768]{1,0:T(8,128)(2,1)S(1)} %get-tuple-element., ...), kind=kLoop, calls=%fused_computation.76 | loop fusion | flops 15915264 | bytes 31890432 | tf_op jit(solution)/shard_map/reduce_sum | solution.py:81
  139.9 2.6 stack.127
  142.6 7.1 fusion.72
  151.0 6.1 fusion.88
  158.3 6.1 fusion.86
  164.5 4.4 fusion.1
  171.6 2.6 convert_reduce_fusion.1
  174.2 3.1 all-reduce
  177.9 3.6 fusion.81
  181.6 95.1 %all-reduce.5.cloned.1.call-done = f32[31,768]{1,0:T(8,128)} async-done(((f32[31,768]{1,0:T(8,128)}), f32[31,768]{1,0:T(8,128)}) %all-reduce.5.cloned.1.call-update) | async-done | bytes 95248 | tf_op jit(solution)/shard_map/psum | solution.py:92
  276.7 363.2 %reduce-scatter.14.cloned.1.call-done = f32[768,24]{0,1:T(8,128)} async-done(((f32[768,1536]{0,1:T(8,128)}), f32[768,24]{0,1:T(8,128)}) %reduce-scatter.14.cloned.1.call-update) | async-done | bytes 73744 | tf_op jit(solution)/shard_map/reduce_scatter | solution.py:118
  639.9 360.7 %reduce-scatter.10.cloned.1.call-done = f32[24,768]{1,0:T(8,128)} async-done(((f32[1536,768]{1,0:T(8,128)}), f32[24,768]{1,0:T(8,128)}) %reduce-scatter.10.cloned.1.call-update) | async-done | bytes 73744 | tf_op jit(solution)/shard_map/reduce_scatter | solution.py:116
  1000.6 360.6 %reduce-scatter.12.cloned.1.call-done = f32[24,768]{1,0:T(8,128)} async-done(((f32[1536,768]{1,0:T(8,128)}), f32[24,768]{1,0:T(8,128)}) %reduce-scatter.12.cloned.1.call-update) | async-done | bytes 73744 | tf_op jit(solution)/shard_map/reduce_scatter | solution.py:117
  (274 shorter events, 28.0 us)
Async XLA Ops:
  7.2 18.6 %all-gather.5.cloned.1.call-start = ((), (), s32[]{:S(2)}) async-start(), calls=%async_computation.11 | async-start | bytes 3538944 | tf_op jit(solution)/shard_map/all_gather | solution.py:40
  7.9 50.0 %all-gather.7.cloned.1.call-start = ((), (), s32[]{:S(2)}) async-start(), calls=%async_computation.12 | async-start | bytes 3538944 | tf_op jit(solution)/shard_map/all_gather | solution.py:66
  8.7 160.3 %reduce-scatter.6.cloned.1.call-start = ((), (), s32[]{:S(2)}) async-start(), calls=%async_computation.5 | async-start | bytes 3538944 | tf_op jit(solution)/shard_map/reduce_scatter | solution.py:61
  9.6 34.8 %copy-start.13 = (f32[768]{0:T(1024)}, f32[768]{0:T(1024)S(1)}, u32[]{:S(2)}) copy-start(f32[768]{0:T(1024)S(1)} %get-tuple-element.47) | copy-start | bytes 9220
  9.6 34.8 %copy-start.15 = (f32[768]{0:T(1024)}, f32[768]{0:T(1024)S(1)}, u32[]{:S(2)}) copy-start(f32[768]{0:T(1024)S(1)} %get-tuple-element.48) | copy-start | bytes 9220
  9.6 34.8 %copy-start.17 = (f32[768]{0:T(1024)}, f32[768]{0:T(1024)S(1)}, u32[]{:S(2)}) copy-start(f32[768]{0:T(1024)S(1)} %get-tuple-element.49) | copy-start | bytes 9220
  9.6 34.8 %copy-start.19 = (f32[768]{0:T(1024)}, f32[768]{0:T(1024)S(1)}, u32[]{:S(2)}) copy-start(f32[768]{0:T(1024)S(1)} %get-tuple-element.50) | copy-start | bytes 9220
  9.6 34.8 %copy-start.21 = (f32[768]{0:T(1024)}, f32[768]{0:T(1024)S(1)}, u32[]{:S(2)}) copy-start(f32[768]{0:T(1024)S(1)} %get-tuple-element.51) | copy-start | bytes 9220
  9.6 34.8 %copy-start.23 = (f32[768]{0:T(1024)}, f32[768]{0:T(1024)S(1)}, u32[]{:S(2)}) copy-start(f32[768]{0:T(1024)S(1)} %get-tuple-element.52) | copy-start | bytes 9220
  9.6 34.8 %copy-start.25 = (f32[768]{0:T(1024)}, f32[768]{0:T(1024)S(1)}, u32[]{:S(2)}) copy-start(f32[768]{0:T(1024)S(1)} %get-tuple-element.53) | copy-start | bytes 9220
  9.6 34.8 %copy-start.27 = (f32[768]{0:T(1024)}, f32[768]{0:T(1024)S(1)}, u32[]{:S(2)}) copy-start(f32[768]{0:T(1024)S(1)} %get-tuple-element.54) | copy-start | bytes 9220
  9.7 34.8 %copy-start.29 = (f32[768]{0:T(1024)}, f32[768]{0:T(1024)S(1)}, u32[]{:S(2)}) copy-start(f32[768]{0:T(1024)S(1)} %get-tuple-element.55) | copy-start | bytes 9220
  9.7 34.8 %copy-start.31 = (f32[768]{0:T(1024)}, f32[768]{0:T(1024)S(1)}, u32[]{:S(2)}) copy-start(f32[768]{0:T(1024)S(1)} %get-tuple-element.56) | copy-start | bytes 9220
  9.7 34.8 %copy-start.33 = (f32[768]{0:T(1024)}, f32[768]{0:T(1024)S(1)}, u32[]{:S(2)}) copy-start(f32[768]{0:T(1024)S(1)} %get-tuple-element.57) | copy-start | bytes 9220
  9.7 34.8 %copy-start.35 = (f32[768]{0:T(1024)}, f32[768]{0:T(1024)S(1)}, u32[]{:S(2)}) copy-start(f32[768]{0:T(1024)S(1)} %get-tuple-element.58) | copy-start | bytes 9220
  34.9 5.0 collective-permute-start
  38.4 5.7 collective-permute-start.1
  95.1 9.5 collective-permute-start.2
  99.0 6.0 collective-permute-start.3
  104.3 67.3 %reduce-scatter.8.cloned.1.call-start = ((), (), s32[]{:S(2)}) async-start(), calls=%async_computation.6 | async-start | bytes 3538944 | tf_op jit(solution)/shard_map/reduce_scatter | solution.py:96
  123.5 153.2 %all-reduce.5.cloned.1.call-start = ((), (), s32[]{:S(2)}) async-start(), calls=%async_computation.9 | async-start | bytes 196608 | tf_op jit(solution)/shard_map/psum | solution.py:92
  142.5 497.4 %reduce-scatter.14.cloned.1.call-start = ((), (), s32[]{:S(2)}) async-start(), calls=%async_computation.10 | async-start | bytes 4792320 | tf_op jit(solution)/shard_map/reduce_scatter | solution.py:118
  149.8 850.8 %reduce-scatter.10.cloned.1.call-start = ((), (), s32[]{:S(2)}) async-start(), calls=%async_computation.7 | async-start | bytes 4792320 | tf_op jit(solution)/shard_map/reduce_scatter | solution.py:116
  157.1 1204.1 %reduce-scatter.12.cloned.1.call-start = ((), (), s32[]{:S(2)}) async-start(), calls=%async_computation.8 | async-start | bytes 4792320 | tf_op jit(solution)/shard_map/reduce_scatter | solution.py:117
  (86 other events, 871.8 us)
Sparse Core Ops, SparseCore 0:
  9.7 16.1 all-gather.4
  27.5 14.9 all-gather.6
  104.4 19.5 reduce-scatter.5
  126.2 18.9 reduce-scatter.7
  150.3 126.3 all-reduce.4
  279.5 360.3 reduce-scatter.13
  642.9 357.6 reduce-scatter.9
  1003.5 357.6 reduce-scatter.11
where the time goes:
time: 1370 us
  waiting for transfers between devices  1200 us (88%)
  other arithmetic  82.8 us (6%)
  matrix products  41.6 us (3%)
  between operations  16.6 us (1%)
    reduce_scatter x1, waiting for transfers between devices, shards(): lax.psum_scatter(out_term, ('seq', 'dp'), scatter_dimension=1, tiled=True)  363 us
    reduce_scatter x1, waiting for transfers between devices, shards(): lax.psum_scatter(value_term, ('seq', 'dp'), scatter_dimension=0, tiled=True)  361 us
    reduce_scatter x1, waiting for transfers between devices, shards(): lax.psum_scatter(gate_term, ('seq', 'dp'), scatter_dimension=0, tiled=True)  361 us
    psum x1, waiting for transfers between devices, shards(): kernel_grad = lax.psum(kernel_term, ('seq', 'dp'))  95.1 us
    reduce_sum x2, other arithmetic, shards(): jnp.sum(padded[offset:offset + count] * slope, axis=0)  42.4 us
  transfers between devices with their start and end apart: 12, of which 7 were waited for; matrix products, arithmetic and copies ran while one was open for 7% of the time, Pallas kernels for 0%

commit v1 on v0

--- a/solution.py
+++ b/solution.py
@@ -89,7 +89,9 @@
     dgates = (dhidden * values * sigma * (1.0 - sigma)).astype(jnp.bfloat16)
     value_term = jnp.dot(normalized_rows.T, dvalues, preferred_element_type=jnp.float32)
     gate_term = jnp.dot(normalized_rows.T, dgates, preferred_element_type=jnp.float32)
-    kernel_grad = lax.psum(kernel_term, ("seq", "dp"))
+    kernel_grad = kernel_term
+    for over in ("seq", "dp"):
+        kernel_grad = lax.psum(kernel_grad, over)
     dnormed_part = jnp.dot(dvalues, w_value.T, preferred_element_type=jnp.float32) + jnp.dot(
         dgates, w_gate.T, preferred_element_type=jnp.float32
     )

time: 1370 us -> 1610 us (1.18)
  waiting for transfers between devices: 1200 us -> 1430 us
  local copies, waits for them, and re-layouts: 8.21 us -> 30.3 us
    psum x1 -> x2, waiting for transfers between devices: 95.1 us -> 315 us  [shards(): kernel_grad = lax.psum(kernel_grad, over)]
    another operation x32, local copies, waits for them, and re-layouts: 2.72 us -> 23.7 us  [shards(): jnp.stack([jnp.sum(padded[offset:offset + count] * slope, axis=0) for off...]
  transfers between devices with their start and end apart: 12 -> 13, of which waited for: 7 -> 8; matrix products, arithmetic and copies ran while one was open for 7% -> 5% of each run, Pallas kernels for 0% -> 0%
where the time goes in v1:
time: 1610 us; the launch traced here: 1600 us
  waiting for transfers between devices  1430 us (89%)
  other arithmetic  70.7 us (4%)
  matrix products  43.7 us (3%)
  local copies, waits for them, and re-layouts  30.3 us (2%)
    reduce_scatter x1, waiting for transfers between devices, shards(): lax.psum_scatter(out_term, ('seq', 'dp'), scatter_dimension=1, tiled=True)  367 us
    reduce_scatter x1, waiting for transfers between devices, shards(): lax.psum_scatter(gate_term, ('seq', 'dp'), scatter_dimension=0, tiled=True)  361 us
    reduce_scatter x1, waiting for transfers between devices, shards(): lax.psum_scatter(value_term, ('seq', 'dp'), scatter_dimension=0, tiled=True)  361 us
    psum x2, waiting for transfers between devices, shards(): kernel_grad = lax.psum(kernel_grad, over)  315 us
  transfers between devices with their start and end apart: 13, of which 8 were waited for; matrix products, arithmetic and copies ran while one was open for 5% of the time, Pallas kernels for 0%

profile of v1, /device:TPU:0, one launch (start us, length us, event | category | flops | bytes accessed | tf_op | source)
XLA Modules:
  0.0 1604.3 jit_solution(5334378828020343096)
XLA Ops:
  10.8 15.1 all-gather.5.cloned.1.call-done
  31.4 3.6 multiply_convert_fusion.3
  35.1 3.5 collective-permute-start
  41.2 3.1 collective-permute-done.1
  44.7 10.8 fusion.94
  58.2 7.0 fusion.93
  67.7 25.7 %fusion.39 = (f32[768]{0:T(1024)S(1)}, f32[768]{0:T(1024)S(1)}, f32[768]{0:T(1024)S(1)}, f32[768]{0:T(1024)S(1)}, f32[768]{0:T(1024)S(1)}, /*index=5*/f32[768]{0...) fusion(f32[798,768]{1,0:T(8,128)} %copy-done.1, ...), kind=kLoop, calls=%fused_computation.77 | loop fusion | flops 25938432 | bytes 48433152 | tf_op jit(solution)/shard_map/reduce_sum | solution.py:81
  93.4 3.9 fusion.38
  116.1 5.4 stack.127
  121.6 4.0 collective-permute-start.2
  126.9 6.3 convolution_convert_fusion
  135.2 10.9 multiply_convert_fusion
  148.5 3.6 add_convert_fusion
  152.4 293.5 %all-reduce.6.cloned.1.call-done = f32[31,768]{1,0:T(8,128)} async-done(((f32[31,768]{1,0:T(8,128)}), f32[31,768]{1,0:T(8,128)}) %all-reduce.6.cloned.1.call-update) | async-done | bytes 95248 | tf_op jit(solution)/shard_map/psum | solution.py:94
  446.0 6.8 fusion.72
  453.5 6.1 fusion.88
  460.8 6.1 fusion.86
  467.0 4.4 fusion.1
  478.4 3.1 all-reduce
  482.2 3.6 fusion.81
  485.9 21.5 %all-reduce.8.cloned.1.call-done = f32[31,768]{1,0:T(8,128)} async-done(((f32[31,768]{1,0:T(8,128)}), f32[31,768]{1,0:T(8,128)}) %all-reduce.8.cloned.1.call-update) | async-done | bytes 95248 | tf_op jit(solution)/shard_map/psum | solution.py:94
  507.3 367.1 %reduce-scatter.14.cloned.1.call-done = f32[768,24]{0,1:T(8,128)} async-done(((f32[768,1536]{0,1:T(8,128)}), f32[768,24]{0,1:T(8,128)}) %reduce-scatter.14.cloned.1.call-update) | async-done | bytes 73744 | tf_op jit(solution)/shard_map/reduce_scatter | solution.py:120
  874.5 360.9 %reduce-scatter.10.cloned.1.call-done = f32[24,768]{1,0:T(8,128)} async-done(((f32[1536,768]{1,0:T(8,128)}), f32[24,768]{1,0:T(8,128)}) %reduce-scatter.10.cloned.1.call-update) | async-done | bytes 73744 | tf_op jit(solution)/shard_map/reduce_scatter | solution.py:118
  1235.3 360.9 %reduce-scatter.12.cloned.1.call-done = f32[24,768]{1,0:T(8,128)} async-done(((f32[1536,768]{1,0:T(8,128)}), f32[24,768]{1,0:T(8,128)}) %reduce-scatter.12.cloned.1.call-update) | async-done | bytes 73744 | tf_op jit(solution)/shard_map/reduce_scatter | solution.py:119
  (237 shorter events, 51.9 us)
Async XLA Ops:
  7.2 24.2 %copy-start = (bf16[1536,768]{1,0:T(8,128)(2,1)S(1)}, bf16[1536,768]{1,0:T(8,128)(2,1)}, u32[]{:S(2)}) copy-start(bf16[1536,768]{1,0:T(8,128)(2,1)} %param.10) | copy-start | bytes 7077892
  7.2 18.6 %all-gather.5.cloned.1.call-start = ((), (), s32[]{:S(2)}) async-start(), calls=%async_computation.12 | async-start | bytes 3538944 | tf_op jit(solution)/shard_map/all_gather | solution.py:40
  7.9 50.2 %all-gather.7.cloned.1.call-start = ((), (), s32[]{:S(2)}) async-start(), calls=%async_computation.13 | async-start | bytes 3538944 | tf_op jit(solution)/shard_map/all_gather | solution.py:66
  8.7 437.2 %all-reduce.6.cloned.1.call-start = ((), (), s32[]{:S(2)}) async-start(), calls=%async_computation.9 | async-start | bytes 196608 | tf_op jit(solution)/shard_map/psum | solution.py:94
  9.4 19.5 %copy-start.10 = (f32[31,768]{1,0:T(8,128)}, f32[31,768]{1,0:T(8,128)S(1)}, u32[]{:S(2)}) copy-start(f32[31,768]{1,0:T(8,128)S(1)} %convert_element_type.70) | copy-start | bytes 285700
  35.1 6.1 collective-permute-start
  38.6 5.7 collective-permute-start.1
  41.1 14.4 copy-start.44
  41.1 14.4 copy-start.46
  41.1 14.4 copy-start.48
  41.1 14.4 copy-start.50
  41.1 14.4 copy-start.52
  41.1 14.4 copy-start.54
  67.6 25.7 %copy-start.2 = (f32[798,768]{1,0:T(8,128)S(1)}, f32[798,768]{1,0:T(8,128)}, u32[]{:S(2)}) copy-start(f32[798,768]{1,0:T(8,128)} %copy-done.1) | copy-start | bytes 7354372
  121.6 349.9 %reduce-scatter.6.cloned.1.call-start = ((), (), s32[]{:S(2)}) async-start(), calls=%async_computation.5 | async-start | bytes 3538944 | tf_op jit(solution)/shard_map/reduce_scatter | solution.py:61
  121.6 11.9 collective-permute-start.2
  125.6 7.9 collective-permute-start.3
  133.2 342.7 %reduce-scatter.8.cloned.1.call-start = ((), (), s32[]{:S(2)}) async-start(), calls=%async_computation.6 | async-start | bytes 3538944 | tf_op jit(solution)/shard_map/reduce_scatter | solution.py:98
  152.1 293.9 %copy-start.73 = (f32[768]{0:T(1024)S(1)}, f32[768]{0:T(1024)}, u32[]{:S(2)}) copy-start(f32[768]{0:T(1024)} %copy-done.72) | copy-start | bytes 9220
  152.1 293.9 %copy-start.75 = (f32[768]{0:T(1024)S(1)}, f32[768]{0:T(1024)}, u32[]{:S(2)}) copy-start(f32[768]{0:T(1024)} %copy-done.74) | copy-start | bytes 9220
  152.1 355.2 %all-reduce.8.cloned.1.call-start = ((), (), s32[]{:S(2)}) async-start(), calls=%async_computation.10 | async-start | bytes 196608 | tf_op jit(solution)/shard_map/psum | solution.py:94
  445.9 428.5 %reduce-scatter.14.cloned.1.call-start = ((), (), s32[]{:S(2)}) async-start(), calls=%async_computation.11 | async-start | bytes 4792320 | tf_op jit(solution)/shard_map/reduce_scatter | solution.py:120
  452.9 782.5 %reduce-scatter.10.cloned.1.call-start = ((), (), s32[]{:S(2)}) async-start(), calls=%async_computation.7 | async-start | bytes 4792320 | tf_op jit(solution)/shard_map/reduce_scatter | solution.py:118
  459.6 1136.6 %reduce-scatter.12.cloned.1.call-start = ((), (), s32[]{:S(2)}) async-start(), calls=%async_computation.8 | async-start | bytes 4792320 | tf_op jit(solution)/shard_map/reduce_scatter | solution.py:119
  (67 other events, 342.5 us)
Sparse Core Ops, SparseCore 0:
  9.7 16.1 all-gather.4
  27.5 14.9 all-gather.6
  121.7 324.1 all-reduce.5
  448.1 11.4 reduce-scatter.5
  461.8 14.0 reduce-scatter.7
  478.2 29.0 all-reduce.7
  510.3 364.1 reduce-scatter.13
  877.4 357.8 reduce-scatter.9
  1238.3 357.8 reduce-scatter.11
